TPU v7x, 32 devices: a whole 2x2x4 slice. The times are simulated.
32 devices in a mesh: row: 8 (over y, x, core), col: 4 (over z).
Axes of the slice: x: 2, y: 2, z: 4, core: 2. Of those that a mesh axis runs over, the one named last changes fastest.
Arguments:
- inverse: float32 [4096, 4096], P('row', 'col'), may hold values from -0.05 to 0.05
- owner: int32 [32], replicated, may hold values from 0 to 31, each once
- struct_parent: int32 [32], replicated, may hold values 0 or 1
- struct_child: int32 [32], replicated, may hold values 0 or 1
- panel_parent: float32 [4096, 1024], P('row', 'col'), may hold values from -1.5 to 1.5
- panel_child: float32 [4096, 1024], P('row', 'col'), may hold values from -1.5 to 1.5
- child_on_parent: float32 [1024, 1024], P('col'), may hold values from -0.1875 to 0.1875
- dinv_parent: float32 [1024, 1024], P('col'), may hold values from -6 to 6
- dinv_child: float32 [1024, 1024], P('col'), may hold values from -6 to 6
Outputs:
- row_parent: float32 [1024, 4096], P('col', 'row')
- inv_parent: float32 [1024, 1024], P('col')
- row_child: float32 [1024, 4096], P('col', 'row')
- inv_cross: float32 [1024, 1024], P('col')
- inv_child: float32 [1024, 1024], P('col')
Inputs may be any that keep to these rules, and one draw needn't show every extreme that they name: `owner`: each slot holds a different block.
All inputs are finite; a program needn't handle non-finite values.
Results may differ from a plain program's by a relative error of at most 0.000071.
Values sent between devices are 32-bit elements; how exact they have to be, the bound alone decides.
A program may use at most 128 MiB of HBM per device.

v0:
```python
import jax
import jax.numpy as jnp
from jax import lax
from jax.sharding import PartitionSpec as P

BLOCK_ROWS = 128


HIGHEST = lax.Precision.HIGHEST


def broadcast(block, axis, source):
    block = jnp.where(lax.axis_index(axis) == source, block, jnp.zeros_like(block))
    return lax.psum(block, axis)


def contract_first(left, right):
    return lax.dot_general(
        left, right, (((0,), (0,)), ((), ())), precision=HIGHEST, preferred_element_type=jnp.float32
    )


def contract_cross(left, right):
    return lax.dot_general(
        left, right, (((0,), (1,)), ((), ())), precision=HIGHEST, preferred_element_type=jnp.float32
    )


def matmul(left, right):
    return jnp.dot(left, right, precision=HIGHEST, preferred_element_type=jnp.float32)


def per_device(
    inverse,
    owner,
    struct_parent,
    struct_child,
    panel_parent,
    panel_child,
    child_on_parent,
    dinv_parent,
    dinv_child,
):
    rows_dev = inverse.shape[0]
    nblocks = owner.shape[0]
    ratio = lax.axis_size("row") // lax.axis_size("col")
    row_at = lax.axis_index("row")
    col_at = lax.axis_index("col")
    row_tiles = rows_dev // BLOCK_ROWS
    matches = owner[:, None] == jnp.arange(nblocks, dtype=jnp.int32)[None, :]
    live_parent = jnp.sum(jnp.where(matches, struct_parent[None, :], 0), axis=1)
    live_child = live_parent * jnp.sum(jnp.where(matches, struct_child[None, :], 0), axis=1)
    parent_rowblk = lax.dynamic_slice_in_dim(live_parent, row_at * row_tiles, row_tiles)
    child_rowblk = lax.dynamic_slice_in_dim(live_child, row_at * row_tiles, row_tiles)
    mask_parent = jnp.repeat(parent_rowblk.astype(jnp.float32), BLOCK_ROWS)
    mask_child = jnp.repeat(child_rowblk.astype(jnp.float32), BLOCK_ROWS)
    masked_parent = panel_parent * mask_parent[:, None]
    masked_child = panel_child * mask_child[:, None]
    full_parent, full_child = (
        lax.all_gather(masked_parent, "col", axis=1, tiled=True),
        lax.all_gather(masked_child, "col", axis=1, tiled=True),
    )
    parent_pieces = []
    child_pieces = []
    for offset in range(ratio):
        got_parent, got_child = (
            broadcast(full_parent, "row", ratio * col_at + offset),
            broadcast(full_child, "row", ratio * col_at + offset),
        )
        parent_pieces.append(got_parent)
        child_pieces.append(got_child)
    column_parent = jnp.concatenate(parent_pieces, axis=0)
    column_child = jnp.concatenate(child_pieces, axis=0)

    def region_term(panel):
        return contract_cross(panel, inverse)

    row_parent = (
        -lax.psum_scatter(region_term(column_parent), "col", scatter_dimension=0, tiled=True)
        * mask_parent[None, :]
    )
    sum_parent, sum_cross = lax.psum(
        (matmul(row_parent, full_parent), matmul(row_parent, full_child)), "row"
    )
    inv_parent = dinv_parent - sum_parent
    parent_full = lax.all_gather(child_on_parent, "col", axis=0, tiled=True)
    inv_cross = -(sum_cross + matmul(inv_parent, parent_full))
    row_child = (
        -lax.psum_scatter(
            region_term(column_child) + contract_first(child_on_parent, row_parent),
            "col",
            scatter_dimension=0,
            tiled=True,
        )
        * mask_child[None, :]
    )
    sum_child = lax.psum(matmul(row_child, full_child), "row")
    cross_term = lax.psum_scatter(
        contract_first(inv_cross, child_on_parent), "col", scatter_dimension=0, tiled=True
    )
    inv_child = dinv_child - sum_child - cross_term
    return (row_parent, inv_parent, row_child, inv_cross, inv_child)


def solution(mesh):
    return jax.shard_map(
        per_device,
        mesh=mesh,
        in_specs=(
            P("row", "col"),
            P(),
            P(),
            P(),
            P("row", "col"),
            P("row", "col"),
            P("col", None),
            P("col", None),
            P("col", None),
        ),
        out_specs=(
            P("col", "row"),
            P("col", None),
            P("col", "row"),
            P("col", None),
            P("col", None),
        ),
        check_vma=False,
    )
```

profile of v0, /device:TPU:0, one launch (start us, length us, event | category | flops | bytes accessed | tf_op | source)
XLA Modules:
  0.0 599.8 jit_solution(15787337251794330934)
XLA Ops:
  7.2 1.0 select_reduce_fusion
  8.4 2.0 broadcast_multiply_fusion
  10.6 2.0 broadcast_multiply_fusion.1
  12.7 46.3 %all-gather.6.cloned.1.call-done = f32[512,1024]{1,0:T(8,128)} async-done(((f32[512,256]{1,0:T(8,128)}), f32[512,1024]{1,0:T(8,128)}) %all-gather.6.cloned.1.call-update) | async-done | bytes 2097168 | tf_op jit(solution)/shard_map/all_gather | solution.py:61
  58.9 4.2 broadcast_select_fusion.1
  63.2 42.4 %all-gather.4.cloned.1.call-done = f32[512,1024]{1,0:T(8,128)} async-done(((f32[512,256]{1,0:T(8,128)}), f32[512,1024]{1,0:T(8,128)}) %all-gather.4.cloned.1.call-update) | async-done | bytes 2097168 | tf_op jit(solution)/shard_map/all_gather | solution.py:60
  105.6 4.2 broadcast_select_fusion.3
  109.9 125.1 %all-reduce.7.cloned.1.call-done = (f32[512,1024]{1,0:T(8,128)}, f32[512,1024]{1,0:T(8,128)}, f32[512,1024]{1,0:T(8,128)}, f32[512,1024]{1,0:T(8,128)}) async-done(((f32[512,1024]{1,0:T(8,128)}, f32[512,1024]{1,0:T(8,128)}, f32[512,1024]{1,0:T(8,128)}, f32[512,1024]{1,0:T(8,128)}), (f32[512,1024]{1,0:T(8,128)}, f32[512,1024]{1,0:T(8,128)}, f32[512,1024]{1,0:T(8,128)}, ...) | async-done | bytes 8388624 | tf_op jit(solution)/shard_map/psum | solution.py:14
  235.0 16.0 %fusion = f32[1024,512]{1,0:T(8,128)} fusion(f32[512,1024]{1,0:T(8,128)S(1)} %copy-done, f32[512,1024]{1,0:T(8,128)} %get-tuple-element.10, f32[512,1024]{1,0:T(8,128)} %get-tuple-element.11), kind=kOutput, calls=%fused_computation | convolution fusion | flops 6443499520 | bytes 8388608 | tf_op jit(solution)/shard_map/dot_general | solution.py:24
  251.0 0.2 reduce-scatter.6.cloned.1.call-start
  251.2 16.1 %fusion.4 = f32[1024,512]{1,0:T(8,128)} fusion(f32[512,1024]{1,0:T(8,128)S(1)} %copy-done, f32[512,1024]{1,0:T(8,128)} %get-tuple-element.12, f32[512,1024]{1,0:T(8,128)} %get-tuple-element.13), kind=kOutput, calls=%fused_computation.4 | convolution fusion | flops 6443499520 | bytes 8388608 | tf_op jit(solution)/shard_map/dot_general | solution.py:24
  267.3 27.6 %reduce-scatter.4.cloned.1.call-done = f32[256,512]{1,0:T(8,128)} async-done(((f32[1024,512]{1,0:T(8,128)}), f32[256,512]{1,0:T(8,128)}) %reduce-scatter.4.cloned.1.call-update) | async-done | bytes 524304 | tf_op jit(solution)/shard_map/reduce_scatter | solution.py:79
  294.9 1.1 negate_multiply_fusion.1
  296.0 0.8 copy-done.4
  296.8 4.9 bitcast_add_fusion
  301.7 0.3 all-reduce.5.cloned.1.call-start
  302.0 0.7 copy-done.5
  302.7 4.6 fusion.12
  307.3 2.9 fusion.11
  310.2 34.5 %reduce-scatter.6.cloned.1.call-done = f32[256,512]{1,0:T(8,128)} async-done(((f32[1024,512]{1,0:T(8,128)}), f32[256,512]{1,0:T(8,128)}) %reduce-scatter.6.cloned.1.call-update) | async-done | bytes 524304 | tf_op jit(solution)/shard_map/reduce_scatter | solution.py:89
  344.7 1.1 negate_multiply_fusion
  345.8 0.8 copy-done.8
  346.6 4.5 fusion.13
  351.1 0.7 all-gather.8.cloned.1.call-update
  351.9 68.0 %all-reduce.5.cloned.1.call-done = (f32[256,1024]{1,0:T(8,128)}, f32[256,1024]{1,0:T(8,128)}, f32[256,1024]{1,0:T(8,128)}) async-done(((f32[256,1024]{1,0:T(8,128)}, f32[256,1024]{1,0:T(8,128)}, f32[256,1024]{1,0:T(8,128)}), (f32[256,1024]{1,0:T(8,128)}, f32[256,1024]{1,0:T(8,128)}, f32[256,1024]{1,0:T(8,128)})) %all-reduce.5.cloned.1.call-update) | async-done | bytes 3145744 | tf_op jit(solution)/shard_map/psum | solution.py:82
  419.9 1.7 sub.9
  421.5 80.7 %all-gather.8.cloned.1.call-done = f32[1024,1024]{1,0:T(8,128)} async-done(((f32[256,1024]{1,0:T(8,128)}), f32[1024,1024]{1,0:T(8,128)}) %all-gather.8.cloned.1.call-update) | async-done | bytes 4194320 | tf_op jit(solution)/shard_map/all_gather | solution.py:86
  502.3 6.3 %fusion.8 = f32[256,1024]{1,0:T(8,128)S(1)} fusion(f32[256,1024]{1,0:T(8,128)} %get-tuple-element.8, f32[256,1024]{1,0:T(8,128)S(1)} %sub.9, f32[1024,1024]{1,0:T(8,128)} %all-gather.8.cloned.1.call-done), kind=kOutput, calls=%fused_computation.10 | convolution fusion | flops 3221749760 | bytes 7340032 | tf_op jit(solution)/shard_map/dot_general | solution.py:30
  508.6 1.0 copy-done.7
  509.6 5.1 fusion.14
  514.7 75.4 %reduce-scatter.8.cloned.1.call-done = f32[256,1024]{1,0:T(8,128)} async-done(((f32[1024,1024]{1,0:T(8,128)}), f32[256,1024]{1,0:T(8,128)}) %reduce-scatter.8.cloned.1.call-update) | async-done | bytes 1048592 | tf_op jit(solution)/shard_map/reduce_scatter | solution.py:98
  590.1 2.8 subtract_subtract_fusion
  (34 shorter events, 0.7 us)
Async XLA Ops:
  7.2 227.8 %copy-start = (f32[512,1024]{1,0:T(8,128)S(1)}, f32[512,1024]{1,0:T(8,128)}, u32[]{:S(2)}) copy-start(f32[512,1024]{1,0:T(8,128)} %param.9) | copy-start | bytes 6291460
  7.2 51.8 %all-gather.6.cloned.1.call-start = ((), (), s32[]{:S(2)}) async-start(), calls=%async_computation.5 | async-start | bytes 2621440 | tf_op jit(solution)/shard_map/all_gather | solution.py:61
  10.4 95.2 %all-gather.4.cloned.1.call-start = ((), (), s32[]{:S(2)}) async-start(), calls=%async_computation.3 | async-start | bytes 2621440 | tf_op jit(solution)/shard_map/all_gather | solution.py:60
  12.6 222.4 %all-reduce.7.cloned.1.call-start = ((), (), s32[]{:S(2)}) async-start(), calls=%async_computation.10 | async-start | bytes 16777216 | tf_op jit(solution)/shard_map/psum | solution.py:14
  109.8 185.1 %reduce-scatter.4.cloned.1.call-start = ((), (), s32[]{:S(2)}) async-start(), calls=%async_computation.4 | async-start | bytes 2621440 | tf_op jit(solution)/shard_map/reduce_scatter | solution.py:79
  251.0 93.7 %reduce-scatter.6.cloned.1.call-start = ((), (), s32[]{:S(2)}) async-start(), calls=%async_computation.6 | async-start | bytes 2621440 | tf_op jit(solution)/shard_map/reduce_scatter | solution.py:89
  251.2 45.6 %copy-start.1 = (f32[256,1024]{1,0:T(8,128)S(1)}, f32[256,1024]{1,0:T(8,128)}, u32[]{:S(2)}) copy-start(f32[256,1024]{1,0:T(8,128)} %param.15) | copy-start | bytes 3145732
  296.0 0.8 copy-start.4
  301.7 1.0 copy-start.5
  301.7 118.1 %all-reduce.5.cloned.1.call-start = ((), (), s32[]{:S(2)}) async-start(), calls=%async_computation.9 | async-start | bytes 6291456 | tf_op jit(solution)/shard_map/psum | solution.py:82
  302.7 4.6 copy-start.3
  345.8 0.8 copy-start.8
  351.1 151.2 %all-gather.8.cloned.1.call-start = ((), (), s32[]{:S(2)}) async-start(), calls=%async_computation.7 | async-start | bytes 5242880 | tf_op jit(solution)/shard_map/all_gather | solution.py:86
  351.8 238.3 %reduce-scatter.8.cloned.1.call-start = ((), (), s32[]{:S(2)}) async-start(), calls=%async_computation.8 | async-start | bytes 5242880 | tf_op jit(solution)/shard_map/reduce_scatter | solution.py:98
  421.5 87.1 %copy-start.6 = (f32[256,1024]{1,0:T(8,128)}, f32[256,1024]{1,0:T(8,128)S(1)}, u32[]{:S(2)}) copy-start(f32[256,1024]{1,0:T(8,128)S(1)} %sub.9) | copy-start | bytes 3145732
  502.3 7.3 %copy-start.2 = (f32[256,1024]{1,0:T(8,128)S(1)}, f32[256,1024]{1,0:T(8,128)}, u32[]{:S(2)}) copy-start(f32[256,1024]{1,0:T(8,128)} %param.15) | copy-start | bytes 3145732
  508.6 1.0 copy-start.7
  514.7 75.5 %copy-start.9 = (f32[256,1024]{1,0:T(8,128)S(1)}, f32[256,1024]{1,0:T(8,128)}, u32[]{:S(2)}) copy-start(f32[256,1024]{1,0:T(8,128)} %param.17) | copy-start | bytes 3145732
Sparse Core Ops, SparseCore 0:
  10.5 48.3 all-gather.5
  61.1 44.4 all-gather.3
  109.9 125.0 all-reduce.6
  251.1 43.7 reduce-scatter.3
  301.8 42.8 reduce-scatter.5
  351.2 68.6 all-reduce.4
  421.4 80.8 all-gather.7
  514.8 75.2 reduce-scatter.7
where the time goes:
time: 600 us
  waiting for transfers between devices  501 us (84%)
  matrix products  60.2 us (10%)
  other arithmetic  20.2 us (3%)
  between operations  14.3 us (2%)
    psum x1, waiting for transfers between devices, broadcast(): return lax.psum(block, axis)  125 us
    all_gather x1, waiting for transfers between devices, per_device(): parent_full = lax.all_gather(child_on_parent, 'col', axis=0, tiled=True)  80.7 us
    reduce_scatter x1, waiting for transfers between devices, per_device(): lax.psum_scatter(contract_first(inv_cross, child_on_parent), 'col', scatt...  75.4 us
    psum x1, waiting for transfers between devices, per_device(): lax.psum((matmul(row_parent, full_parent), matmul(row_parent, full_child)...  68 us
    all_gather x1, waiting for transfers between devices, per_device(): lax.all_gather(masked_child, 'col', axis=1, tiled=True)  46.3 us
    all_gather x1, waiting for transfers between devices, per_device(): lax.all_gather(masked_parent, 'col', axis=1, tiled=True)  42.4 us
    reduce_scatter x1, waiting for transfers between devices, per_device(): lax.psum_scatter(region_term(column_child) + contract_first(child_on_pare...  34.5 us
    dot_general x2, matrix products, contract_cross(): lax.dot_general(left, right, (((0,), (1,)), ((), ())), precision=HIGHEST,...  32 us
  transfers between devices with their start and end apart: 8, of which 8 were waited for; matrix products, arithmetic and copies ran while one was open for 5% of the time, Pallas kernels for 0%

commit v1 on v0

v1 whole, which is shorter than its diff:
```python
import jax
import jax.numpy as jnp
from jax import lax
from jax.sharding import PartitionSpec as P

BLOCK_ROWS = 128
PRECISION = lax.Precision.HIGH


def contract(left, right, left_dim, right_dim):
    return lax.dot_general(
        left,
        right,
        (((left_dim,), (right_dim,)), ((), ())),
        precision=PRECISION,
        preferred_element_type=jnp.float32,
    )


def per_device(
    inverse,
    owner,
    struct_parent,
    struct_child,
    panel_parent,
    panel_child,
    child_on_parent,
    dinv_parent,
    dinv_child,
):
    rows_dev = inverse.shape[0]
    nblocks = owner.shape[0]
    rows, cols = lax.axis_size("row"), lax.axis_size("col")
    ratio = rows // cols
    width = child_on_parent.shape[1]
    chunk = width // cols
    row_at = lax.axis_index("row")
    row_tiles = rows_dev // BLOCK_ROWS
    matches = owner[:, None] == jnp.arange(nblocks, dtype=jnp.int32)[None, :]
    live_parent = jnp.sum(jnp.where(matches, struct_parent[None, :], 0), axis=1)
    live_child = live_parent * jnp.sum(jnp.where(matches, struct_child[None, :], 0), axis=1)
    parent_rowblk = lax.dynamic_slice_in_dim(live_parent, row_at * row_tiles, row_tiles)
    child_rowblk = lax.dynamic_slice_in_dim(live_child, row_at * row_tiles, row_tiles)
    mask_parent = jnp.repeat(parent_rowblk.astype(jnp.float32), BLOCK_ROWS)
    mask_child = jnp.repeat(child_rowblk.astype(jnp.float32), BLOCK_ROWS)
    masked_parent = panel_parent * mask_parent[:, None]
    masked_child = panel_child * mask_child[:, None]

    swap = [
        ((ratio * a + k) * cols + b, (ratio * b + k) * cols + a)
        for a in range(cols)
        for b in range(cols)
        for k in range(ratio)
    ]

    def column_panel(tile):
        moved = lax.ppermute(tile, ("row", "col"), swap)
        got = lax.all_gather(moved, "row", axis=0, tiled=True)
        return got.reshape(cols, ratio * rows_dev, chunk)

    def region_term(panel):
        return contract(panel, inverse, 1, 1)

    term_parent = region_term(column_panel(masked_parent))
    term_child = region_term(column_panel(masked_child))
    parent_full = lax.all_gather(child_on_parent, "col", axis=0, tiled=True)
    full_parent = lax.all_gather(masked_parent, "col", axis=1, tiled=True)
    full_child = lax.all_gather(masked_child, "col", axis=1, tiled=True)

    lower = contract(parent_full, term_parent.reshape(width, rows_dev), 0, 0)
    term_both = term_child.reshape(width, rows_dev) - lower
    row_parent = (
        -lax.psum_scatter(
            term_parent.reshape(width, rows_dev), "col", scatter_dimension=0, tiled=True
        )
        * mask_parent[None, :]
    )
    row_child = (
        -lax.psum_scatter(term_both, "col", scatter_dimension=0, tiled=True) * mask_child[None, :]
    )
    sum_parent, sum_cross, sum_child = lax.psum(
        (
            contract(row_parent, full_parent, 1, 0),
            contract(row_parent, full_child, 1, 0),
            contract(row_child, full_child, 1, 0),
        ),
        "row",
    )
    inv_parent = dinv_parent - sum_parent
    inv_cross = -(sum_cross + contract(inv_parent, parent_full, 1, 0))
    cross_column = lax.all_to_all(inv_cross, "col", split_axis=1, concat_axis=0, tiled=True)
    inv_child = dinv_child - sum_child - contract(cross_column, parent_full, 0, 0)
    return (row_parent, inv_parent, row_child, inv_cross, inv_child)


def solution(mesh):
    return jax.shard_map(
        per_device,
        mesh=mesh,
        in_specs=(
            P("row", "col"),
            P(),
            P(),
            P(),
            P("row", "col"),
            P("row", "col"),
            P("col", None),
            P("col", None),
            P("col", None),
        ),
        out_specs=(
            P("col", "row"),
            P("col", None),
            P("col", "row"),
            P("col", None),
            P("col", None),
        ),
        check_vma=False,
    )
```

time: 600 us -> 549 us (0.915)
  waiting for transfers between devices: 501 us -> 447 us
  blocking collectives: 0 us -> 30.3 us
  matrix products: 60.2 us -> 35.2 us
  other arithmetic: 20.2 us -> 7.15 us
  local copies, waits for them, and re-layouts: 3.47 us -> 11.9 us
    all_gather x2 -> x4, waiting for transfers between devices: 88.7 us -> 222 us  [the longest x2 135 us: column_panel(): got = lax.all_gather(moved, 'row', axis=0, tiled=True)]
    psum x2 -> x1, waiting for transfers between devices: 193 us -> 68.8 us  [per_device(): lax.psum((contract(row_parent, full_parent, 1, 0), contract(row_parent, f...]
    reduce_scatter x3 -> x2, waiting for transfers between devices: 138 us -> 84 us  [the longest x1 43.9 us: per_device(): lax.psum_scatter(term_parent.reshape(width, rows_dev), 'col', scatter_dim...]
    all_to_all x0 -> x1, blocking collectives: none -> 30.3 us  [per_device(): lax.all_to_all(inv_cross, 'col', split_axis=1, concat_axis=0, tiled=True)]
    dot_general x8, matrix products: 60.2 us -> 35.2 us  [contract(): lax.dot_general(left, right, (((left_dim,), (right_dim,)), ((), ())), pre...]
    all_gather x1, waiting for transfers between devices: 80.7 us -> 69.9 us  [per_device(): parent_full = lax.all_gather(child_on_parent, 'col', axis=0, tiled=True)]
    dot_general x0 -> x2, local copies, waits for them, and re-layouts: none -> 10.8 us  [contract(): lax.dot_general(left, right, (((left_dim,), (right_dim,)), ((), ())), pre...]
    select_n x2 -> x0, other arithmetic: 8.46 us -> none  [broadcast(): jnp.where(lax.axis_index(axis) == source, block, jnp.zeros_like(block))]
  transfers between devices with their start and end apart: 8 -> 10, of which waited for: 8 -> 8; matrix products, arithmetic and copies ran while one was open for 5% -> 5% of each run, Pallas kernels for 0% -> 0%
where the time goes in v1:
time: 549 us
  waiting for transfers between devices  447 us (81%)
  matrix products  35.2 us (6%)
  blocking collectives  30.3 us (6%)
  between operations  14.3 us (3%)
  local copies, waits for them, and re-layouts  11.9 us (2%)
  other arithmetic  7.15 us (1%)
    all_gather x2, waiting for transfers between devices, column_panel(): got = lax.all_gather(moved, 'row', axis=0, tiled=True)  135 us
    all_gather x1, waiting for transfers between devices, per_device(): parent_full = lax.all_gather(child_on_parent, 'col', axis=0, tiled=True)  69.9 us
    psum x1, waiting for transfers between devices, per_device(): lax.psum((contract(row_parent, full_parent, 1, 0), contract(row_parent, f...  68.8 us
    all_gather x1, waiting for transfers between devices, per_device(): full_child = lax.all_gather(masked_child, 'col', axis=1, tiled=True)  45.8 us
    reduce_scatter x1, waiting for transfers between devices, per_device(): lax.psum_scatter(term_parent.reshape(width, rows_dev), 'col', scatter_dim...  43.9 us
    all_gather x1, waiting for transfers between devices, per_device(): full_parent = lax.all_gather(masked_parent, 'col', axis=1, tiled=True)  40.8 us
    reduce_scatter x1, waiting for transfers between devices, per_device(): lax.psum_scatter(term_both, 'col', scatter_dimension=0, tiled=True)  40.1 us
    dot_general x8, matrix products, contract(): lax.dot_general(left, right, (((left_dim,), (right_dim,)), ((), ())), pre...  35.2 us
  transfers between devices with their start and end apart: 10, of which 8 were waited for; matrix products, arithmetic and copies ran while one was open for 5% of the time, Pallas kernels for 0%

profile of v1, /device:TPU:0, one launch (start us, length us, event | category | flops | bytes accessed | tf_op | source)
XLA Modules:
  0.0 548.6 jit_solution(2519168364760123978)
XLA Ops:
  7.2 1.0 select_reduce_fusion
  8.4 1.2 broadcast_multiply_fusion.1
  9.6 0.7 collective-permute-start
  10.3 0.8 copy-done.14
  11.3 1.2 broadcast_multiply_fusion
  12.5 1.5 collective-permute-start.1
  14.1 0.7 all-gather.12.cloned.1.call-update
  14.8 102.1 %all-gather.6.cloned.1.call-done = f32[4096,256]{1,0:T(8,128)} async-done(((f32[512,256]{1,0:T(8,128)}), f32[4096,256]{1,0:T(8,128)}) %all-gather.6.cloned.1.call-update) | async-done | bytes 4194320 | tf_op jit(solution)/shard_map/all_gather | solution.py:58
  116.9 5.4 copy.21
  122.3 33.1 %all-gather.10.cloned.1.call-done = f32[4096,256]{1,0:T(8,128)} async-done(((f32[512,256]{1,0:T(8,128)}), f32[4096,256]{1,0:T(8,128)}) %all-gather.10.cloned.1.call-update) | async-done | bytes 4194320 | tf_op jit(solution)/shard_map/all_gather | solution.py:58
  155.4 5.4 copy.22
  160.8 7.0 %fusion.1 = f32[1024,512]{1,0:T(8,128)} fusion(f32[1024,1024]{1,0:T(8,128)} %bitcast.38, f32[512,1024]{1,0:T(8,128)S(1)} %copy-done), kind=kOutput, calls=%fused_computation.16 | convolution fusion | flops 3221225472 | bytes 8388608 | tf_op jit(solution)/shard_map/dot_general | solution.py:11
  167.8 69.9 %all-gather.12.cloned.1.call-done = f32[1024,1024]{1,0:T(8,128)} async-done(((f32[256,1024]{1,0:T(8,128)}), f32[1024,1024]{1,0:T(8,128)}) %all-gather.12.cloned.1.call-update) | async-done | bytes 4194320 | tf_op jit(solution)/shard_map/all_gather | solution.py:66
  237.8 6.1 %fusion.3 = f32[512,1024]{0,1:T(8,128)S(1)} fusion(f32[1024,512]{1,0:T(8,128)} %fusion.1, f32[1024,1024]{1,0:T(8,128)} %all-gather.12.cloned.1.call-done), kind=kOutput, calls=%fused_computation.18 | convolution fusion | flops 3221225472 | bytes 8388608 | tf_op jit(solution)/shard_map/dot_general | solution.py:11
  243.9 4.8 bitcast_subtract_fusion
  248.8 0.5 reduce-scatter.3.cloned.1.call-update
  249.4 0.5 all-gather.14.cloned.1.call-update
  249.9 0.7 all-gather.8.cloned.1.call-update
  250.9 40.1 %reduce-scatter.5.cloned.1.call-done = f32[256,512]{1,0:T(8,128)} async-done(((f32[1024,512]{1,0:T(8,128)}), f32[256,512]{1,0:T(8,128)}) %reduce-scatter.5.cloned.1.call-update) | async-done | bytes 524304 | tf_op jit(solution)/shard_map/reduce_scatter | solution.py:79
  291.0 1.1 negate_multiply_fusion
  292.1 43.9 %reduce-scatter.3.cloned.1.call-done = f32[256,512]{1,0:T(8,128)} async-done(((f32[1024,512]{1,0:T(8,128)}), f32[256,512]{1,0:T(8,128)}) %reduce-scatter.3.cloned.1.call-update) | async-done | bytes 524304 | tf_op jit(solution)/shard_map/reduce_scatter | solution.py:73
  336.0 1.1 negate_multiply_fusion.1
  337.1 45.8 %all-gather.14.cloned.1.call-done = f32[512,1024]{1,0:T(8,128)} async-done(((f32[512,256]{1,0:T(8,128)}), f32[512,1024]{1,0:T(8,128)}) %all-gather.14.cloned.1.call-update) | async-done | bytes 2097168 | tf_op jit(solution)/shard_map/all_gather | solution.py:68
  382.9 3.8 fusion.5
  386.7 2.1 fusion.4
  388.7 40.8 %all-gather.8.cloned.1.call-done = f32[512,1024]{1,0:T(8,128)} async-done(((f32[512,256]{1,0:T(8,128)}), f32[512,1024]{1,0:T(8,128)}) %all-gather.8.cloned.1.call-update) | async-done | bytes 2097168 | tf_op jit(solution)/shard_map/all_gather | solution.py:67
  429.5 3.6 fusion.2
  433.2 68.8 %all-reduce.3.cloned.1.call-done = (f32[256,1024]{1,0:T(8,128)}, f32[256,1024]{1,0:T(8,128)}, f32[256,1024]{1,0:T(8,128)}) async-done(((f32[256,1024]{1,0:T(8,128)}, f32[256,1024]{1,0:T(8,128)}, f32[256,1024]{1,0:T(8,128)}), (f32[256,1024]{1,0:T(8,128)}, f32[256,1024]{1,0:T(8,128)}, f32[256,1024]{1,0:T(8,128)})) %all-reduce.3.cloned.1.call-update) | async-done | bytes 3145744 | tf_op jit(solution)/shard_map/psum | solution.py:81
  502.0 1.4 sub.12
  503.5 4.6 fusion
  508.3 30.3 %all_to_all.19 = f32[256,4,256]{2,0,1:T(8,128)S(1)} all-to-all(f32[256,4,256]{2,0,1:T(8,128)S(1)} %bitcast.42), channel_id=1, replica_groups=mesh['row'=8,'col'=4] {'col'}, dimensions={1} | all-to-all | bytes 2097152 | tf_op jit(solution)/shard_map/all_to_all | solution.py:91
  538.6 3.2 convolution_subtract_fusion
  (49 shorter events, 1.1 us)
Async XLA Ops:
  7.2 153.7 %copy-start = (f32[512,1024]{1,0:T(8,128)S(1)}, f32[512,1024]{1,0:T(8,128)}, u32[]{:S(2)}) copy-start(f32[512,1024]{1,0:T(8,128)} %param.9) | copy-start | bytes 6291460
  7.2 109.8 %all-gather.6.cloned.1.call-start = ((), (), s32[]{:S(2)}) async-start(), calls=%async_computation.3 | async-start | bytes 4718592 | tf_op jit(solution)/shard_map/all_gather | solution.py:58
  9.6 112.8 %copy-start.8 = (f32[512,256]{1,0:T(8,128)}, f32[512,256]{1,0:T(8,128)S(1)}, u32[]{:S(2)}) copy-start(f32[512,256]{1,0:T(8,128)S(1)} %broadcast_multiply_fusion.1) | copy-start | bytes 1572868
  9.6 0.7 collective-permute-start
  10.3 0.8 copy-start.14
  11.1 144.3 %all-gather.10.cloned.1.call-start = ((), (), s32[]{:S(2)}) async-start(), calls=%async_computation.6 | async-start | bytes 4718592 | tf_op jit(solution)/shard_map/all_gather | solution.py:58
  12.5 109.8 %copy-start.9 = (f32[512,256]{1,0:T(8,128)}, f32[512,256]{1,0:T(8,128)S(1)}, u32[]{:S(2)}) copy-start(f32[512,256]{1,0:T(8,128)S(1)} %broadcast_multiply_fusion) | copy-start | bytes 1572868
  12.5 1.5 collective-permute-start.1
  14.0 223.8 %all-gather.12.cloned.1.call-start = ((), (), s32[]{:S(2)}) async-start(), calls=%async_computation.7 | async-start | bytes 5242880 | tf_op jit(solution)/shard_map/all_gather | solution.py:66
  14.8 276.2 %reduce-scatter.5.cloned.1.call-start = ((), (), s32[]{:S(2)}) async-start(), calls=%async_computation.8 | async-start | bytes 2621440 | tf_op jit(solution)/shard_map/reduce_scatter | solution.py:79
  237.8 6.1 %copy-start.2 = (f32[4,256,1024]{2,1,0:T(8,128)S(1)}, f32[4,256,1024]{2,1,0:T(8,128)}, u32[]{:S(2)}) copy-start(f32[4,256,1024]{2,1,0:T(8,128)} %copy.22) | copy-start | bytes 12582916
  248.7 87.3 %reduce-scatter.3.cloned.1.call-start = ((), (), s32[]{:S(2)}) async-start(), calls=%async_computation.4 | async-start | bytes 2621440 | tf_op jit(solution)/shard_map/reduce_scatter | solution.py:73
  249.3 133.6 %all-gather.14.cloned.1.call-start = ((), (), s32[]{:S(2)}) async-start(), calls=%async_computation.9 | async-start | bytes 2621440 | tf_op jit(solution)/shard_map/all_gather | solution.py:68
  249.9 179.6 %all-gather.8.cloned.1.call-start = ((), (), s32[]{:S(2)}) async-start(), calls=%async_computation.5 | async-start | bytes 2621440 | tf_op jit(solution)/shard_map/all_gather | solution.py:67
  250.6 251.3 %all-reduce.3.cloned.1.call-start = ((), (), s32[]{:S(2)}) async-start(), calls=%async_computation.10 | async-start | bytes 6291456 | tf_op jit(solution)/shard_map/psum | solution.py:81
  292.1 94.6 %copy-start.7 = (f32[256,512]{1,0:T(8,128)}, f32[256,512]{1,0:T(8,128)S(1)}, u32[]{:S(2)}) copy-start(f32[256,512]{1,0:T(8,128)S(1)} %negate_multiply_fusion) | copy-start | bytes 1572868
  337.1 92.4 %copy-start.4 = (f32[256,512]{1,0:T(8,128)}, f32[256,512]{1,0:T(8,128)S(1)}, u32[]{:S(2)}) copy-start(f32[256,512]{1,0:T(8,128)S(1)} %negate_multiply_fusion.1) | copy-start | bytes 1572868
  382.9 3.8 copy-start.3
  433.1 68.8 %copy-start.10 = (f32[256,1024]{1,0:T(8,128)S(1)}, f32[256,1024]{1,0:T(8,128)}, u32[]{:S(2)}) copy-start(f32[256,1024]{1,0:T(8,128)} %param.16) | copy-start | bytes 3145732
  502.0 1.5 copy-start.11
  503.4 4.7 copy-start.5
  503.5 35.0 %copy-start.12 = (f32[256,1024]{1,0:T(8,128)S(1)}, f32[256,1024]{1,0:T(8,128)}, u32[]{:S(2)}) copy-start(f32[256,1024]{1,0:T(8,128)} %param.17) | copy-start | bytes 3145732
  503.5 35.0 %copy-start.13 = (f32[256,1024]{1,0:T(8,128)S(1)}, f32[256,1024]{1,0:T(8,128)}, u32[]{:S(2)}) copy-start(f32[256,1024]{1,0:T(8,128)} %get-tuple-element.9) | copy-start | bytes 3145732
  508.1 30.4 %copy-start.6 = (f32[256,1024]{1,0:T(8,128)}, f32[256,1024]{1,0:T(8,128)S(1)}, u32[]{:S(2)}) copy-start(f32[256,1024]{1,0:T(8,128)S(1)} %fusion) | copy-start | bytes 3145732
  508.2 30.4 %copy-start.1 = (f32[1024,1024]{1,0:T(8,128)S(1)}, f32[1024,1024]{1,0:T(8,128)}, u32[]{:S(2)}) copy-start(f32[1024,1024]{1,0:T(8,128)} %all-gather.12.cloned.1.call-done) | copy-start | bytes 12582916
Sparse Core Ops, SparseCore 0:
  11.2 105.6 all-gather.5
  118.8 36.5 all-gather.9
  157.0 80.7 all-gather.11
  248.8 42.1 reduce-scatter.4
  293.1 42.8 reduce-scatter.2
  338.0 44.8 all-gather.13
  385.0 44.4 all-gather.7
  433.6 68.2 all-reduce.2

commit v2 on v1

--- a/solution.py
+++ b/solution.py
@@ -1,6 +1,10 @@
+import functools
+
 import jax
 import jax.numpy as jnp
 from jax import lax
+from jax.experimental import pallas as pl
+from jax.experimental.pallas import tpu as pltpu
 from jax.sharding import PartitionSpec as P
 
 BLOCK_ROWS = 128
@@ -15,6 +19,160 @@
         precision=PRECISION,
         preferred_element_type=jnp.float32,
     )
+
+
+def exchange_kernel(
+    rows, cols, lp, lc, cop, gp, gc, fp, fc, hp,
+    t_send, t_recv, z_send, z_recv, r_send, r_recv, f_send, f_recv, c_send, c_recv, l_sem,
+):
+    chips = rows // 2
+    row, col = lax.axis_index("row"), lax.axis_index("col")
+    chip, core = row // 2, row % 2
+    other = chip * 2 + (1 - core)
+    swap_row, swap_col = col * 2 + core, chip
+    off_diagonal = chip != col
+    chunk = lp.shape[1]
+    part = cop.shape[0]
+    half = part // 2
+
+    def remote(src, dst, send, recv, to):
+        return pltpu.make_async_remote_copy(
+            src_ref=src, dst_ref=dst, send_sem=send, recv_sem=recv,
+            device_id=to, device_id_type=pl.DeviceIdType.MESH,
+        )
+
+    def columns(ref, at):
+        return ref.at[:, pl.ds(pl.multiple_of(at * chunk, 128), chunk)]
+
+    def half_rows(ref, at, which):
+        return ref.at[pl.ds(pl.multiple_of(at * part + which * half, 8), half)]
+
+    def greet(to):
+        pl.semaphore_signal(barrier, inc=1, device_id=to, device_id_type=pl.DeviceIdType.MESH)
+
+    barrier = pltpu.get_barrier_semaphore()
+    for j in range(1, cols):
+        greet((row, (col + j) % cols))
+    for j in range(1, chips):
+        greet((((chip + j) % chips) * 2 + core, col))
+    greet((other, col))
+    pl.when(off_diagonal)(lambda: greet((swap_row, swap_col)))
+    pl.semaphore_wait(barrier, cols - 1 + chips - 1 + 1 + off_diagonal.astype(jnp.int32))
+
+    tiles, columns_out, fulls = (lp, lc), (gp, gc), (fp, fc)
+
+    def swap(p):
+        return remote(
+            tiles[p], columns_out[p].at[swap_row], t_send.at[p], t_recv.at[p], (swap_row, swap_col)
+        )
+
+    def swap_local(p):
+        return pltpu.make_async_copy(tiles[p], columns_out[p].at[row], l_sem.at[3 + p])
+
+    for p in range(2):
+        pl.when(off_diagonal)(lambda p=p: swap(p).start())
+        pl.when(jnp.logical_not(off_diagonal))(lambda p=p: swap_local(p).start())
+
+    locals_ = [pltpu.make_async_copy(tiles[p], columns(fulls[p], col), l_sem.at[p]) for p in range(2)]
+    locals_.append(
+        pltpu.make_async_copy(
+            cop, hp.at[pl.ds(pl.multiple_of(col * part, 8), part)], l_sem.at[2]
+        )
+    )
+    for copy in locals_:
+        copy.start()
+
+    def along_panel(p, j, at):
+        return remote(
+            tiles[p], columns(fulls[p], at), z_send.at[p, j], z_recv.at[p, j],
+            (row, (col + j) % cols),
+        )
+
+    def along_block(j, at):
+        return remote(
+            cop.at[pl.ds(pl.multiple_of(core * half, 8), half)], half_rows(hp, at, core),
+            z_send.at[2, j], z_recv.at[2, j], (row, (col + j) % cols),
+        )
+
+    for j in range(1, cols):
+        along_block(j, col).start()
+    for p in range(2):
+        for j in range(1, cols):
+            along_panel(p, j, col).start()
+
+    def across(p, j, slot):
+        return remote(
+            columns_out[p].at[row], columns_out[p].at[slot], r_send.at[p, j], r_recv.at[p, j],
+            (((chip + j) % chips) * 2 + core, col),
+        )
+
+    def hand(p, j, slot):
+        return remote(
+            columns_out[p].at[slot], columns_out[p].at[slot], f_send.at[p, j], f_recv.at[p, j],
+            (other, col),
+        )
+
+    for p in range(2):
+        pl.when(off_diagonal)(lambda p=p: swap(p).wait_recv())
+        pl.when(jnp.logical_not(off_diagonal))(lambda p=p: swap_local(p).wait())
+        for j in range(1, chips):
+            across(p, j, row).start()
+        hand(p, 0, row).start()
+    for p in range(2):
+        for j in range(1, chips):
+            slot = ((chip - j + chips) % chips) * 2 + core
+            across(p, j, slot).wait_recv()
+            hand(p, j, slot).start()
+
+    def hand_block(j, which):
+        block = half_rows(hp, (col - j + cols) % cols, which)
+        return remote(block, block, c_send.at[j], c_recv.at[j], (other, col))
+
+    for j in range(1, cols):
+        along_block(j, (col - j + cols) % cols).wait_recv()
+        hand_block(j, core).start()
+    for p in range(2):
+        for j in range(1, cols):
+            along_panel(p, j, (col - j + cols) % cols).wait_recv()
+    for j in range(1, cols):
+        hand_block(j, 1 - core).wait_recv()
+        hand_block(j, core).wait_send()
+        along_block(j, col).wait_send()
+    for p in range(2):
+        for j in range(1, cols):
+            along_panel(p, j, col).wait_send()
+        for j in range(chips):
+            chip_from = (chip - j + chips) % chips
+            hand(p, j, chip_from * 2 + (1 - core)).wait_recv()
+            hand(p, j, chip_from * 2 + core).wait_send()
+            if j:
+                across(p, j, row).wait_send()
+        pl.when(off_diagonal)(lambda p=p: swap(p).wait_send())
+    for copy in locals_:
+        copy.wait()
+
+
+def exchange(lp, lc, cop, rows, cols):
+    size, chunk = lp.shape
+    part, width = cop.shape
+    chips = rows // 2
+    sem = pltpu.SemaphoreType.DMA
+    shape = lambda *dims: jax.ShapeDtypeStruct(dims, jnp.float32)
+    anywhere = pl.BlockSpec(memory_space=pl.ANY)
+    return pl.pallas_call(
+        functools.partial(exchange_kernel, rows, cols),
+        out_shape=(
+            shape(rows, size, chunk), shape(rows, size, chunk),
+            shape(size, width), shape(size, width), shape(width, width),
+        ),
+        in_specs=[anywhere] * 3,
+        out_specs=[anywhere] * 5,
+        scratch_shapes=[
+            sem((2,)), sem((2,)), sem((3, cols)), sem((3, cols)), sem((2, chips)), sem((2, chips)),
+            sem((2, chips)), sem((2, chips)), sem((cols,)), sem((cols,)), sem((5,)),
+        ],
+        compiler_params=pltpu.CompilerParams(collective_id=0, has_side_effects=True),
+    )(lp, lc, cop)
 
 
 def per_device(
@@ -46,27 +204,15 @@
     masked_parent = panel_parent * mask_parent[:, None]
     masked_child = panel_child * mask_child[:, None]
 
-    swap = [
-        ((ratio * a + k) * cols + b, (ratio * b + k) * cols + a)
-        for a in range(cols)
-        for b in range(cols)
-        for k in range(ratio)
-    ]
-
-    def column_panel(tile):
-        moved = lax.ppermute(tile, ("row", "col"), swap)
-        got = lax.all_gather(moved, "row", axis=0, tiled=True)
-        return got.reshape(cols, ratio * rows_dev, chunk)
+    column_parent, column_child, full_parent, full_child, parent_full = exchange(
+        masked_parent, masked_child, child_on_parent, rows, cols
+    )
 
     def region_term(panel):
         return contract(panel, inverse, 1, 1)
 
-    term_parent = region_term(column_panel(masked_parent))
-    term_child = region_term(column_panel(masked_child))
-    parent_full = lax.all_gather(child_on_parent, "col", axis=0, tiled=True)
-    full_parent = lax.all_gather(masked_parent, "col", axis=1, tiled=True)
-    full_child = lax.all_gather(masked_child, "col", axis=1, tiled=True)
-
+    term_parent = region_term(column_parent.reshape(cols, ratio * rows_dev, chunk))
+    term_child = region_term(column_child.reshape(cols, ratio * rows_dev, chunk))
     lower = contract(parent_full, term_parent.reshape(width, rows_dev), 0, 0)
     term_both = term_child.reshape(width, rows_dev) - lower
     row_parent = (

time: 549 us -> 427 us (0.78)
  waiting for transfers between devices: 447 us -> 141 us
  Pallas kernels: 0 us -> 186 us
    all_gather x5 -> x0, waiting for transfers between devices: 292 us -> none  [the longest x2 135 us: column_panel(): got = lax.all_gather(moved, 'row', axis=0, tiled=True)]
    pallas_call x0 -> x1, Pallas kernels: none -> 186 us  [exchange(): pl.pallas_call(functools.partial(exchange_kernel, rows, cols), out_shape=...]
    reshape x0 -> x2, local copies, waits for them, and re-layouts: none -> 10.8 us  [the longest x1 5.42 us: per_device(): column_parent.reshape(cols, ratio * rows_dev, chunk)]
    dot_general x2 -> x0, local copies, waits for them, and re-layouts: 10.8 us -> none  [contract(): lax.dot_general(left, right, (((left_dim,), (right_dim,)), ((), ())), pre...]
    reduce_scatter x1, waiting for transfers between devices: 43.9 us -> 34.3 us  [per_device(): lax.psum_scatter(term_parent.reshape(width, rows_dev), 'col', scatter_dim...]
  transfers between devices with their start and end apart: 10 -> 3, of which waited for: 8 -> 3; matrix products, arithmetic and copies ran while one was open for 5% -> 5% of each run, Pallas kernels for 0% -> 0%
where the time goes in v2:
time: 427 us
  Pallas kernels  186 us (44%)
  waiting for transfers between devices  141 us (33%)
  matrix products  34.8 us (8%)
  blocking collectives  30.3 us (7%)
  between operations  13.9 us (3%)
  local copies, waits for them, and re-layouts  11.2 us (3%)
  other arithmetic  8.99 us (2%)
    pallas_call x1, Pallas kernels, exchange(): pl.pallas_call(functools.partial(exchange_kernel, rows, cols), out_shape=...  186 us
    psum x1, waiting for transfers between devices, per_device(): lax.psum((contract(row_parent, full_parent, 1, 0), contract(row_parent, f...  68.8 us
    reduce_scatter x1, waiting for transfers between devices, per_device(): lax.psum_scatter(term_both, 'col', scatter_dimension=0, tiled=True)  38.1 us
    dot_general x8, matrix products, contract(): lax.dot_general(left, right, (((left_dim,), (right_dim,)), ((), ())), pre...  34.8 us
    reduce_scatter x1, waiting for transfers between devices, per_device(): lax.psum_scatter(term_parent.reshape(width, rows_dev), 'col', scatter_dim...  34.3 us
    all_to_all x1, blocking collectives, per_device(): lax.all_to_all(inv_cross, 'col', split_axis=1, concat_axis=0, tiled=True)  30.3 us
  transfers between devices with their start and end apart: 3, of which 3 were waited for; matrix products, arithmetic and copies ran while one was open for 5% of the time, Pallas kernels for 0%

profile of v2, /device:TPU:0, one launch (start us, length us, event | category | flops | bytes accessed | tf_op | source)
XLA Modules:
  0.0 426.9 jit_solution(13643578718290571568)
XLA Ops:
  7.2 0.0 reduce-scatter.3.cloned.1.call-start
  7.2 1.0 select_reduce_fusion
  8.2 0.1 dynamic-slice_convert_fusion
  8.3 0.1 broadcast_bitcast_fusion
  8.4 0.1 broadcast_bitcast_fusion.1
  8.5 2.0 broadcast_multiply_fusion.1.lp
  10.4 2.0 broadcast_multiply_fusion.lc
  12.4 186.2 %shard_map.128 = (f32[8,512,256]{2,1,0:T(8,128)}, f32[8,512,256]{2,1,0:T(8,128)}, f32[512,1024]{1,0:T(8,128)}, f32[512,1024]{1,0:T(8,128)}, f32[1024,1024]{1,0:T(8,128)}) custom-call(f32[512,256]{1,0:T(8,128)} %broadcast_multiply_fusion.1.lp, f32[512,256]{1,0:T(8,128)} %broadcast_multiply_fusion.lc, f32[256,1024]{1,0:T(8,128)} %cop.1), custom_call_target="tpu_custom_call" | custom-call | tf_op jit(solution)/shard_map/pallas_call | solution.py:162
  198.6 5.4 %copy.17 = f32[4,1024,256]{1,2,0:T(8,128)} copy(f32[4,1024,256]{2,1,0:T(8,128)} %bitcast.39) | data formatting | bytes 8388608 | tf_op jit(solution)/shard_map/reshape | solution.py:214
  204.0 7.0 %fusion.1 = f32[1024,512]{1,0:T(8,128)} fusion(f32[1024,1024]{1,0:T(8,128)} %bitcast.35, f32[512,1024]{1,0:T(8,128)S(1)} %copy-done), kind=kOutput, calls=%fused_computation.16 | convolution fusion | flops 3221225472 | bytes 8388608 | tf_op jit(solution)/shard_map/dot_general | solution.py:15
  211.0 0.0 reduce-scatter.3.cloned.1.call-update
  211.0 0.0 reduce-scatter.5.cloned.1.call-start
  211.1 5.4 %copy.18 = f32[4,1024,256]{1,2,0:T(8,128)} copy(f32[4,1024,256]{2,1,0:T(8,128)} %bitcast.38) | data formatting | bytes 8388608 | tf_op jit(solution)/shard_map/reshape | solution.py:215
  216.5 5.5 %fusion.3 = f32[1024,512]{1,0:T(8,128)S(1)} fusion(f32[1024,1024]{1,0:T(8,128)} %bitcast.36, f32[512,1024]{1,0:T(8,128)S(1)} %copy-done), kind=kOutput, calls=%fused_computation.18 | convolution fusion | flops 3221225472 | bytes 8388608 | tf_op jit(solution)/shard_map/dot_general | solution.py:15
  222.0 4.8 %convolution_subtract_fusion = f32[1024,512]{1,0:T(8,128)} fusion(f32[1024,512]{1,0:T(8,128)S(1)} %fusion.3, f32[1024,1024]{1,0:T(8,128)S(1)} %copy-done.1, f32[1024,512]{1,0:T(8,128)S(1)} %copy-done.3), kind=kOutput, calls=%fused_computation | convolution fusion | flops 3221749760 | bytes 10485760 | tf_op jit(solution)/shard_map/dot_general | solution.py:15
  226.8 0.0 reduce-scatter.5.cloned.1.call-update
  226.8 0.2 all-reduce.3.cloned.1.call-start
  227.1 34.3 %reduce-scatter.3.cloned.1.call-done = f32[256,512]{1,0:T(8,128)} async-done(((f32[1024,512]{1,0:T(8,128)}), f32[256,512]{1,0:T(8,128)}) %reduce-scatter.3.cloned.1.call-update) | async-done | bytes 524304 | tf_op jit(solution)/shard_map/reduce_scatter | solution.py:219
  261.3 1.1 negate_multiply_fusion.1
  262.5 3.9 fusion.2
  266.3 2.1 fusion.4
  268.4 38.1 %reduce-scatter.5.cloned.1.call-done = f32[256,512]{1,0:T(8,128)} async-done(((f32[1024,512]{1,0:T(8,128)}), f32[256,512]{1,0:T(8,128)}) %reduce-scatter.5.cloned.1.call-update) | async-done | bytes 524304 | tf_op jit(solution)/shard_map/reduce_scatter | solution.py:225
  306.5 1.1 negate_multiply_fusion
  307.6 3.8 fusion.5
  311.4 0.0 all-reduce.3.cloned.1.call-update
  311.5 68.8 %all-reduce.3.cloned.1.call-done = (f32[256,1024]{1,0:T(8,128)}, f32[256,1024]{1,0:T(8,128)}, f32[256,1024]{1,0:T(8,128)}) async-done(((f32[256,1024]{1,0:T(8,128)}, f32[256,1024]{1,0:T(8,128)}, f32[256,1024]{1,0:T(8,128)}), (f32[256,1024]{1,0:T(8,128)}, f32[256,1024]{1,0:T(8,128)}, f32[256,1024]{1,0:T(8,128)})) %all-reduce.3.cloned.1.call-update) | async-done | bytes 3145744 | tf_op jit(solution)/shard_map/psum | solution.py:227
  380.2 1.8 sub.12
  382.0 0.1 copy-done.9
  382.1 4.6 %fusion = f32[256,1024]{1,0:T(8,128)S(1)} fusion(f32[256,1024]{1,0:T(8,128)S(1)} %copy-done.9, f32[256,1024]{1,0:T(8,128)S(1)} %sub.12, f32[1024,1024]{1,0:T(8,128)} %get-tuple-element.13), kind=kOutput, calls=%fused_computation.3 | convolution fusion | flops 1611137024 | bytes 7340032 | tf_op jit(solution)/shard_map/dot_general | solution.py:15
  386.7 0.1 copy.22
  386.8 30.3 %all_to_all.19 = f32[256,4,256]{2,0,1:T(8,128)S(1)} all-to-all(f32[256,4,256]{2,0,1:T(8,128)S(1)} %bitcast.40), channel_id=1, replica_groups=mesh['row'=8,'col'=4] {'col'}, dimensions={1} | all-to-all | bytes 2097152 | tf_op jit(solution)/shard_map/all_to_all | solution.py:237
  417.1 3.2 convolution_subtract_fusion.1
  (24 shorter events, 0.1 us)
Async XLA Ops:
  7.2 196.9 %copy-start = (f32[512,1024]{1,0:T(8,128)S(1)}, f32[512,1024]{1,0:T(8,128)}, u32[]{:S(2)}) copy-start(f32[512,1024]{1,0:T(8,128)} %param.9) | copy-start | bytes 6291460
  7.2 254.1 %reduce-scatter.3.cloned.1.call-start = ((), (), s32[]{:S(2)}) async-start(), calls=%async_computation.3 | async-start | bytes 2621440 | tf_op jit(solution)/shard_map/reduce_scatter | solution.py:219
  211.0 95.5 %reduce-scatter.5.cloned.1.call-start = ((), (), s32[]{:S(2)}) async-start(), calls=%async_computation.4 | async-start | bytes 2621440 | tf_op jit(solution)/shard_map/reduce_scatter | solution.py:225
  216.5 5.5 %copy-start.1 = (f32[1024,1024]{1,0:T(8,128)S(1)}, f32[1024,1024]{1,0:T(8,128)}, u32[]{:S(2)}) copy-start(f32[1024,1024]{1,0:T(8,128)} %get-tuple-element.13) | copy-start | bytes 12582916
  216.5 5.5 %copy-start.3 = (f32[1024,512]{1,0:T(8,128)S(1)}, f32[1024,512]{1,0:T(8,128)}, u32[]{:S(2)}) copy-start(f32[1024,512]{1,0:T(8,128)} %fusion.1) | copy-start | bytes 6291460
  226.8 153.4 %all-reduce.3.cloned.1.call-start = ((), (), s32[]{:S(2)}) async-start(), calls=%async_computation.5 | async-start | bytes 6291456 | tf_op jit(solution)/shard_map/psum | solution.py:227
  262.4 5.9 %copy-start.5 = (f32[256,512]{1,0:T(8,128)}, f32[256,512]{1,0:T(8,128)S(1)}, u32[]{:S(2)}) copy-start(f32[256,512]{1,0:T(8,128)S(1)} %negate_multiply_fusion.1) | copy-start | bytes 1572868
  262.4 3.9 copy-start.4
  307.6 3.9 copy-start.8
  380.2 1.9 copy-start.9
  382.0 4.7 %copy-start.6 = (f32[256,1024]{1,0:T(8,128)}, f32[256,1024]{1,0:T(8,128)S(1)}, u32[]{:S(2)}) copy-start(f32[256,1024]{1,0:T(8,128)S(1)} %sub.12) | copy-start | bytes 3145732
  382.1 35.0 %copy-start.10 = (f32[256,1024]{1,0:T(8,128)S(1)}, f32[256,1024]{1,0:T(8,128)}, u32[]{:S(2)}) copy-start(f32[256,1024]{1,0:T(8,128)} %param.17) | copy-start | bytes 3145732
  382.1 35.0 %copy-start.11 = (f32[256,1024]{1,0:T(8,128)S(1)}, f32[256,1024]{1,0:T(8,128)}, u32[]{:S(2)}) copy-start(f32[256,1024]{1,0:T(8,128)} %get-tuple-element.19) | copy-start | bytes 3145732
  386.7 30.4 %copy-start.7 = (f32[256,1024]{1,0:T(8,128)}, f32[256,1024]{1,0:T(8,128)S(1)}, u32[]{:S(2)}) copy-start(f32[256,1024]{1,0:T(8,128)S(1)} %fusion) | copy-start | bytes 3145732
  386.7 30.4 %copy-start.2 = (f32[1024,1024]{1,0:T(8,128)S(1)}, f32[1024,1024]{1,0:T(8,128)}, u32[]{:S(2)}) copy-start(f32[1024,1024]{1,0:T(8,128)} %get-tuple-element.13) | copy-start | bytes 12582916
Sparse Core Ops, SparseCore 0:
  211.2 50.1 reduce-scatter.2
  263.6 42.8 reduce-scatter.4
  311.6 68.6 all-reduce.2
